TPU v7x, 256 devices: a whole 4x4x8 slice. The times are simulated.
256 devices in a mesh: dp: 16 (over z, y_hi), row: 4 (over y_lo, core), col: 4 (over x).
Axes of the slice: x: 4, y: 4 (y_hi: 2, y_lo: 2; y = y_hi * 2 + y_lo), z: 8, core: 2. Of those that a mesh axis runs over, the one named last changes fastest.
Arguments:
- tokens: bfloat16 [7168, 4096], P(('dp', 'col'), 'row'), may hold values from -6 to 6
- gate_up: bfloat16 [2, 4096, 14336], P(None, 'row', ('dp', 'col')), may hold values from -0.09375 to 0.09375
- down_weight: bfloat16 [14336, 4096], P(('dp', 'col'), 'row'), may hold values from -0.046875 to 0.046875
Outputs:
- mixed: bfloat16 [7168, 4096], P(('dp', 'col'), 'row')
- col_check: float32 [4096], P('row')
- row_check: float32 [7168], P(('dp', 'col'))
All inputs are finite; a program needn't handle non-finite values.
Results may differ from a plain program's by a relative error of at most 0.0049.
Values may be sent and summed in bfloat16 or wider, within the bound.
No kernel may reach another device: no remote copies, remote signals or barrier semaphores. Data moves between devices by JAX's collectives and lax.ppermute only.
A program may use at most 128 MiB of HBM per device.

v0:
```python
import math
import jax
import jax.numpy as jnp
from jax import lax
from jax.sharding import PartitionSpec as P


def swiglu(partial_value):
    return (jax.nn.silu(partial_value[:, 0]) * partial_value[:, 1]).astype(jnp.bfloat16)


def hidden_units(partial_value):
    share = lax.psum_scatter(partial_value, "row", scatter_dimension=0, tiled=True)
    return lax.all_gather(swiglu(share), "row", axis=0, tiled=True)


def make_accumulate(hidden, shard_piece):
    columns_wide = hidden.astype(jnp.float32)
    piece_wide = shard_piece.astype(jnp.float32)
    output_part = jnp.dot(hidden, shard_piece, preferred_element_type=jnp.float32)
    column_part = jnp.dot(
        jnp.sum(columns_wide, axis=0), piece_wide, precision=lax.Precision.HIGHEST
    )
    row_part = jnp.dot(columns_wide, jnp.sum(piece_wide, axis=1), precision=lax.Precision.HIGHEST)
    return (output_part, column_part, row_part)


def per_device(tokens, gate_up, down_weight):
    total_tokens = tokens.shape[0] * lax.axis_size(("dp", "col"))
    model_width = tokens.shape[1] * lax.axis_size("row")
    group_rows = lax.all_gather(tokens, "col", axis=0, tiled=True)
    partial_value = jnp.einsum(
        "td,gdf->tgf",
        group_rows,
        lax.all_gather(gate_up, "dp", axis=2, tiled=True),
        preferred_element_type=jnp.float32,
    )
    hidden = hidden_units(partial_value)
    output_part, column_part, row_part = make_accumulate(
        hidden, lax.all_gather(down_weight, "dp", axis=0, tiled=True)
    )
    mixed, row_share = (
        lax.psum_scatter(output_part, "col", scatter_dimension=0, tiled=True),
        lax.psum_scatter(row_part, "col", scatter_dimension=0, tiled=True),
    )
    col_check = lax.psum(column_part, ("dp", "col")) / math.sqrt(total_tokens)
    row_check = lax.psum(row_share, "row") / math.sqrt(model_width)
    return (mixed.astype(jnp.bfloat16), col_check, row_check)


def solution(mesh):
    placed = (P(("dp", "col"), "row"), P(None, "row", ("dp", "col")), P(("dp", "col"), "row"))
    return jax.shard_map(
        per_device,
        mesh=mesh,
        in_specs=placed,
        out_specs=(P(("dp", "col"), "row"), P("row"), P(("dp", "col"))),
        check_vma=False,
    )
```

profile of v0, /device:TPU:8, one launch (start us, length us, event | category | flops | bytes accessed | tf_op | source)
XLA Modules:
  0.0 748.7 jit_solution(9035475301600994231)
XLA Ops:
  7.2 0.0 all-gather.4.cloned.1.call-start
  7.2 0.7 all-gather.4.cloned.1.call-update
  7.9 0.0 reduce-scatter.3.cloned.1.call-start
  7.9 14.2 %all_gather.12 = bf16[448,1024]{1,0:T(8,128)(2,1)S(1)} all-gather(bf16[112,1024]{1,0:T(8,128)(2,1)} %param.3), channel_id=1, replica_groups=mesh['dp'=16,'row'=4,'col'=4] {'col'}, dimensions={0}, use_global_device_ids=true | all-gather | bytes 1146880 | tf_op jit(solution)/shard_map/all_gather | solution.py:31
  22.2 192.1 %all-gather.4.cloned.1.call-done = bf16[2,1024,3584]{1,2,0:T(8,128)(2,1)} async-done(((bf16[2,1024,224]{1,2,0:T(8,128)(2,1)}), bf16[2,1024,3584]{1,2,0:T(8,128)(2,1)}) %all-gather.4.cloned.1.call-update) | async-done | bytes 14680080 | tf_op jit(solution)/shard_map/all_gather | solution.py:35
  214.2 22.2 %fusion.2 = f32[448,2,3584]{2,0,1:T(8,128)} fusion(bf16[2,1024,3584]{1,2,0:T(8,128)(2,1)} %all-gather.4.cloned.1.call-done, bf16[448,1024]{1,0:T(8,128)(2,1)S(1)} %all_gather.12), kind=kOutput, calls=%fused_computation.6 | convolution fusion | flops 6576668672 | bytes 28442624 | tf_op jit(solution)/shard_map/td,gdf->tgf/dot_general | solution.py:32
  236.5 0.0 reduce-scatter.3.cloned.1.call-update
  236.5 0.0 all-gather.8.cloned.1.call-start
  236.5 0.7 all-gather.8.cloned.1.call-update
  237.2 0.0 all-gather.6.cloned.1.call-start
  237.3 113.1 %reduce-scatter.3.cloned.1.call-done = f32[112,2,3584]{2,0,1:T(8,128)} async-done(((f32[448,2,3584]{2,0,1:T(8,128)}), f32[112,2,3584]{2,0,1:T(8,128)}) %reduce-scatter.3.cloned.1.call-update) | async-done | bytes 3211280 | tf_op jit(solution)/shard_map/reduce_scatter | solution.py:13
  350.3 3.2 fusion.1
  353.6 0.0 all-gather.6.cloned.1.call-update
  353.6 0.0 copy-start.1
  353.6 0.0 reduce-scatter.5.cloned.1.call-start
  353.6 126.6 %all-gather.8.cloned.1.call-done = bf16[3584,1024]{1,0:T(8,128)(2,1)} async-done(((bf16[224,1024]{1,0:T(8,128)(2,1)}), bf16[3584,1024]{1,0:T(8,128)(2,1)}) %all-gather.8.cloned.1.call-update) | async-done | bytes 7340048 | tf_op jit(solution)/shard_map/all_gather | solution.py:40
  480.3 38.6 %all-gather.6.cloned.1.call-done = bf16[448,3584]{1,0:T(8,128)(2,1)} async-done(((bf16[112,3584]{1,0:T(8,128)(2,1)}), bf16[448,3584]{1,0:T(8,128)(2,1)}) %all-gather.6.cloned.1.call-update) | async-done | bytes 3211280 | tf_op jit(solution)/shard_map/all_gather | solution.py:14
  518.8 8.8 %fusion.4 = f32[448,1024]{1,0:T(8,128)} fusion(bf16[448,3584]{1,0:T(8,128)(2,1)} %all-gather.6.cloned.1.call-done, bf16[3584,1024]{1,0:T(8,128)(2,1)} %all-gather.8.cloned.1.call-done), kind=kOutput, calls=%fused_computation.10 | convolution fusion | flops 3288334336 | bytes 12386304 | tf_op jit(solution)/shard_map/dot_general | solution.py:20
  527.6 0.0 reduce-scatter.5.cloned.1.call-update
  527.6 0.0 copy-done.1
  527.6 0.6 dynamic-slice
  528.9 0.0 copy-start
  528.9 4.3 convert_reduce_fusion
  533.2 0.0 copy-done
  533.2 0.6 convert_reduce_fusion.1
  533.8 2.6 fusion.6
  536.4 10.9 %all-reduce = f32[448]{0:T(512)S(1)} all-reduce(f32[448]{0:T(512)S(1)} %bitcast.24), channel_id=4, replica_groups=mesh['dp'=16,'row'=4,'col'=4] {'col'}, use_global_device_ids=true, to_apply=%region_5.6.clone | all-reduce | flops 448 | bytes 3584
  547.2 0.1 dynamic-slice.1
  547.3 6.5 psum.15
  553.8 5.2 fusion.5
  559.0 180.3 %psum.14 = f32[1024]{0:T(1024)S(1)} all-reduce(f32[1024]{0:T(1024)S(1)} %bitcast.23), channel_id=1, replica_groups=mesh['dp'=16,'row'=4,'col'=4] {'dp','col'}, use_global_device_ids=true, to_apply=%region_3.4 | all-reduce | flops 1024 | bytes 8192 | tf_op jit(solution)/shard_map/psum | solution.py:46
  739.3 0.5 broadcast_multiply_fusion.1
  739.8 0.6 broadcast_multiply_fusion
  740.4 0.0 reduce-scatter.5.cloned.1.call-done
  740.4 1.7 convert_element_type.13
  (2 shorter events, 0.0 us)
Async XLA Ops:
  7.2 207.1 %all-gather.4.cloned.1.call-start = ((), (), s32[]{:S(2)}) async-start(), calls=%async_computation.2 | async-start | bytes 15597568 | tf_op jit(solution)/shard_map/all_gather | solution.py:35
  7.9 342.4 %reduce-scatter.3.cloned.1.call-start = ((), (), s32[]{:S(2)}) async-start(), calls=%async_computation.3 | async-start | bytes 16056320 | tf_op jit(solution)/shard_map/reduce_scatter | solution.py:13
  236.5 243.8 %all-gather.8.cloned.1.call-start = ((), (), s32[]{:S(2)}) async-start(), calls=%async_computation.5 | async-start | bytes 7798784 | tf_op jit(solution)/shard_map/all_gather | solution.py:40
  237.2 281.6 %all-gather.6.cloned.1.call-start = ((), (), s32[]{:S(2)}) async-start(), calls=%async_computation.4 | async-start | bytes 4014080 | tf_op jit(solution)/shard_map/all_gather | solution.py:14
  353.6 174.1 %copy-start.1 = (u32[256]{0:T(256)S(1)}, u32[256]{0:T(256)}, u32[]{:S(2)}) copy-start(u32[256]{0:T(256)} %constant.16) | copy-start | bytes 3076
  353.6 386.8 %reduce-scatter.5.cloned.1.call-start = ((), (), s32[]{:S(2)}) async-start(), calls=%async_computation.6 | async-start | bytes 2293760 | tf_op jit(solution)/shard_map/reduce_scatter | solution.py:43
  528.9 4.3 copy-start
Sparse Core Ops, SparseCore 0:
  10.6 203.5 all-gather.3
  236.6 113.6 reduce-scatter.2
  352.9 127.3 all-gather.7
  481.9 36.8 all-gather.5
  527.7 32.7 reduce-scatter.4
where the time goes:
time: 749 us
  waiting for transfers between devices  472 us (63%)
  blocking collectives  212 us (28%)
  matrix products  38.7 us (5%)
  between operations  14.5 us (2%)
  other arithmetic  10.9 us (1%)
    all_gather x1, waiting for transfers between devices, per_device(): lax.all_gather(gate_up, 'dp', axis=2, tiled=True)  192 us
    psum x1, blocking collectives, per_device(): col_check = lax.psum(column_part, ('dp', 'col')) / math.sqrt(total_tokens)  180 us
    all_gather x1, waiting for transfers between devices, per_device(): lax.all_gather(down_weight, 'dp', axis=0, tiled=True)  127 us
    reduce_scatter x1, waiting for transfers between devices, hidden_units(): lax.psum_scatter(partial_value, 'row', scatter_dimension=0, tiled=True)  113 us
    all_gather x1, waiting for transfers between devices, hidden_units(): return lax.all_gather(swiglu(share), 'row', axis=0, tiled=True)  38.6 us
    dot_general x1, matrix products, per_device(): jnp.einsum('td,gdf->tgf', group_rows, lax.all_gather(gate_up, 'dp', axis=...  22.2 us
  transfers between devices with their start and end apart: 5, of which 4 were waited for; matrix products, arithmetic and copies ran while one was open for 2% of the time, Pallas kernels for 0%

commit v1 on v0

--- a/solution.py
+++ b/solution.py
@@ -43,7 +43,7 @@
         lax.psum_scatter(output_part, "col", scatter_dimension=0, tiled=True),
         lax.psum_scatter(row_part, "col", scatter_dimension=0, tiled=True),
     )
-    col_check = lax.psum(column_part, ("dp", "col")) / math.sqrt(total_tokens)
+    col_check = lax.psum(lax.psum(column_part, "col"), "dp") / math.sqrt(total_tokens)
     row_check = lax.psum(row_share, "row") / math.sqrt(model_width)
     return (mixed.astype(jnp.bfloat16), col_check, row_check)
 

time: 749 us -> 611 us (0.82)
  blocking collectives: 212 us -> 73.6 us
    psum x1 -> x2, blocking collectives: 180 us -> 52.8 us  [the longest x1 41.6 us: per_device(): lax.psum(lax.psum(column_part, 'col'), 'dp') / math.sqrt(total_tokens)]
    unnamed x1 -> x0, blocking collectives: 10.9 us -> none
  transfers between devices with their start and end apart: 5 -> 5, of which waited for: 4 -> 4; matrix products, arithmetic and copies ran while one was open for 2% -> 3% of each run, Pallas kernels for 0% -> 0%
where the time goes in v1:
time: 611 us
  waiting for transfers between devices  472 us (77%)
  blocking collectives  73.6 us (12%)
  matrix products  36.5 us (6%)
  between operations  14.8 us (2%)
  other arithmetic  13 us (2%)
    all_gather x1, waiting for transfers between devices, per_device(): lax.all_gather(gate_up, 'dp', axis=2, tiled=True)  192 us
    all_gather x1, waiting for transfers between devices, per_device(): lax.all_gather(down_weight, 'dp', axis=0, tiled=True)  126 us
    reduce_scatter x1, waiting for transfers between devices, hidden_units(): lax.psum_scatter(partial_value, 'row', scatter_dimension=0, tiled=True)  113 us
    psum x1, blocking collectives, per_device(): lax.psum(lax.psum(column_part, 'col'), 'dp') / math.sqrt(total_tokens)  41.6 us
    all_gather x1, waiting for transfers between devices, hidden_units(): return lax.all_gather(swiglu(share), 'row', axis=0, tiled=True)  38.6 us
    dot_general x1, matrix products, per_device(): jnp.einsum('td,gdf->tgf', group_rows, lax.all_gather(gate_up, 'dp', axis=...  22.2 us
    all_gather x1, blocking collectives, per_device(): group_rows = lax.all_gather(tokens, 'col', axis=0, tiled=True)  14.2 us
  transfers between devices with their start and end apart: 5, of which 4 were waited for; matrix products, arithmetic and copies ran while one was open for 3% of the time, Pallas kernels for 0%

profile of v1, /device:TPU:8, one launch (start us, length us, event | category | flops | bytes accessed | tf_op | source)
XLA Modules:
  0.0 610.7 jit_solution(9749235932446568716)
XLA Ops:
  7.2 0.0 all-gather.4.cloned.1.call-start
  7.2 0.7 all-gather.4.cloned.1.call-update
  7.9 0.0 reduce-scatter.3.cloned.1.call-start
  7.9 14.2 %all_gather.12 = bf16[448,1024]{1,0:T(8,128)(2,1)S(1)} all-gather(bf16[112,1024]{1,0:T(8,128)(2,1)} %param.3), channel_id=1, replica_groups=mesh['dp'=16,'row'=4,'col'=4] {'col'}, dimensions={0}, use_global_device_ids=true | all-gather | bytes 1146880 | tf_op jit(solution)/shard_map/all_gather | solution.py:31
  22.2 192.1 %all-gather.4.cloned.1.call-done = bf16[2,1024,3584]{1,2,0:T(8,128)(2,1)} async-done(((bf16[2,1024,224]{1,2,0:T(8,128)(2,1)}), bf16[2,1024,3584]{1,2,0:T(8,128)(2,1)}) %all-gather.4.cloned.1.call-update) | async-done | bytes 14680080 | tf_op jit(solution)/shard_map/all_gather | solution.py:35
  214.2 22.2 %fusion.2 = f32[448,2,3584]{2,0,1:T(8,128)} fusion(bf16[2,1024,3584]{1,2,0:T(8,128)(2,1)} %all-gather.4.cloned.1.call-done, bf16[448,1024]{1,0:T(8,128)(2,1)S(1)} %all_gather.12), kind=kOutput, calls=%fused_computation.6 | convolution fusion | flops 6576668672 | bytes 28442624 | tf_op jit(solution)/shard_map/td,gdf->tgf/dot_general | solution.py:32
  236.5 0.0 reduce-scatter.3.cloned.1.call-update
  236.5 0.0 all-gather.8.cloned.1.call-start
  236.6 0.7 all-gather.8.cloned.1.call-update
  237.2 0.0 all-gather.6.cloned.1.call-start
  237.3 113.1 %reduce-scatter.3.cloned.1.call-done = f32[112,2,3584]{2,0,1:T(8,128)} async-done(((f32[448,2,3584]{2,0,1:T(8,128)}), f32[112,2,3584]{2,0,1:T(8,128)}) %reduce-scatter.3.cloned.1.call-update) | async-done | bytes 3211280 | tf_op jit(solution)/shard_map/reduce_scatter | solution.py:13
  350.4 3.2 fusion.1
  353.6 0.0 all-gather.6.cloned.1.call-update
  353.6 0.0 copy-start.1
  353.6 0.2 reduce-scatter.5.cloned.1.call-start
  353.8 126.5 %all-gather.8.cloned.1.call-done = bf16[3584,1024]{1,0:T(8,128)(2,1)} async-done(((bf16[224,1024]{1,0:T(8,128)(2,1)}), bf16[3584,1024]{1,0:T(8,128)(2,1)}) %all-gather.8.cloned.1.call-update) | async-done | bytes 7340048 | tf_op jit(solution)/shard_map/all_gather | solution.py:40
  480.3 38.6 %all-gather.6.cloned.1.call-done = bf16[448,3584]{1,0:T(8,128)(2,1)} async-done(((bf16[112,3584]{1,0:T(8,128)(2,1)}), bf16[448,3584]{1,0:T(8,128)(2,1)}) %all-gather.6.cloned.1.call-update) | async-done | bytes 3211280 | tf_op jit(solution)/shard_map/all_gather | solution.py:14
  518.9 8.7 %fusion.4 = f32[448,1024]{1,0:T(8,128)} fusion(bf16[448,3584]{1,0:T(8,128)(2,1)} %all-gather.6.cloned.1.call-done, bf16[3584,1024]{1,0:T(8,128)(2,1)} %all-gather.8.cloned.1.call-done), kind=kOutput, calls=%fused_computation.10 | convolution fusion | flops 3288334336 | bytes 12386304 | tf_op jit(solution)/shard_map/dot_general | solution.py:20
  527.6 0.0 slice-start
  527.6 0.0 reduce-scatter.5.cloned.1.call-update
  527.7 0.0 copy-done.1
  527.7 0.6 dynamic-slice
  529.2 0.0 slice-start.1
  529.2 4.3 convert_reduce_fusion
  533.5 0.0 copy-start
  533.5 2.7 convert_reduce_fusion.1
  536.2 0.2 copy-done
  536.4 2.6 fusion.6
  538.9 0.0 slice-done
  538.9 0.0 slice-done.1
  539.0 2.9 fusion.5
  541.9 11.3 %all-reduce.1 = (f32[1024]{0:T(1024)S(1)}, f32[448]{0:T(512)S(1)}) all-reduce(f32[1024]{0:T(1024)S(1)} %bitcast.25, f32[448]{0:T(512)S(1)} %bitcast.26), channel_id=1, replica_groups=mesh['dp'=16,'row'=4,'col'=4] {'col'}, use_global_device_ids=true, to_apply=%region_3.4 | all-reduce | flops 1472 | bytes 11776 | tf_op jit(solution)/shard_map/psum | solution.py:46
  553.2 0.1 dynamic-slice.1
  553.3 6.5 %psum.23 = f32[112]{0:T(128)S(1)} all-reduce(f32[112]{0:T(128)S(1)} %dynamic-slice.1), channel_id=1, replica_groups=mesh['dp'=16,'row'=4,'col'=4] {'row'}, use_global_device_ids=true, to_apply=%region_7.8 | all-reduce | flops 112 | bytes 896 | tf_op jit(solution)/shard_map/psum | solution.py:47
  559.8 41.6 %psum.22 = f32[1024]{0:T(1024)S(1)} all-reduce(f32[1024]{0:T(1024)S(1)} %get-tuple-element.3), channel_id=1, replica_groups=mesh['dp'=16,'row'=4,'col'=4] {'dp'}, use_global_device_ids=true, to_apply=%region_4.5 | all-reduce | flops 1024 | bytes 8192 | tf_op jit(solution)/shard_map/psum | solution.py:46
  601.3 0.5 broadcast_multiply_fusion.1
  601.8 0.6 broadcast_multiply_fusion
  602.4 0.0 reduce-scatter.5.cloned.1.call-done
  602.4 1.7 convert_element_type.13
  (3 shorter events, 0.0 us)
Async XLA Ops:
  7.2 207.1 %all-gather.4.cloned.1.call-start = ((), (), s32[]{:S(2)}) async-start(), calls=%async_computation.2 | async-start | bytes 15597568 | tf_op jit(solution)/shard_map/all_gather | solution.py:35
  7.9 342.5 %reduce-scatter.3.cloned.1.call-start = ((), (), s32[]{:S(2)}) async-start(), calls=%async_computation.3 | async-start | bytes 16056320 | tf_op jit(solution)/shard_map/reduce_scatter | solution.py:13
  236.5 243.8 %all-gather.8.cloned.1.call-start = ((), (), s32[]{:S(2)}) async-start(), calls=%async_computation.5 | async-start | bytes 7798784 | tf_op jit(solution)/shard_map/all_gather | solution.py:40
  237.2 281.6 %all-gather.6.cloned.1.call-start = ((), (), s32[]{:S(2)}) async-start(), calls=%async_computation.4 | async-start | bytes 4014080 | tf_op jit(solution)/shard_map/all_gather | solution.py:14
  353.6 174.0 %copy-start.1 = (u32[256]{0:T(256)S(1)}, u32[256]{0:T(256)}, u32[]{:S(2)}) copy-start(u32[256]{0:T(256)} %constant.16) | copy-start | bytes 3076
  353.6 248.8 %reduce-scatter.5.cloned.1.call-start = ((), (), s32[]{:S(2)}) async-start(), calls=%async_computation.6 | async-start | bytes 2293760 | tf_op jit(solution)/shard_map/reduce_scatter | solution.py:43
  527.6 11.3 %slice-start = ((s8[7340032]{0:T(1024)(128)(4,1)}), s8[3145728]{0:T(1024)(128)(4,1)S(1)}, s32[]{:S(2)}) async-start(s8[7340032]{0:T(1024)(128)(4,1)} %bitcast.23), calls=%async_computation.7 | async-start | bytes 6291456
  529.2 9.7 %slice-start.1 = ((s8[7340032]{0:T(1024)(128)(4,1)}), s8[4194304]{0:T(1024)(128)(4,1)S(1)}, s32[]{:S(2)}) async-start(s8[7340032]{0:T(1024)(128)(4,1)} %bitcast.23), calls=%async_computation.8 | async-start | bytes 8388608
  533.5 2.9 copy-start
Sparse Core Ops, SparseCore 0:
  10.6 203.5 all-gather.3
  236.6 113.6 reduce-scatter.2
  352.9 127.3 all-gather.7
  482.0 36.8 all-gather.5
  527.8 33.0 reduce-scatter.4

commit v2 on v0

--- a/solution.py
+++ b/solution.py
@@ -32,7 +32,9 @@
     partial_value = jnp.einsum(
         "td,gdf->tgf",
         group_rows,
-        lax.all_gather(gate_up, "dp", axis=2, tiled=True),
+        jnp.concatenate(
+            lax.all_to_all(jnp.stack([gate_up] * lax.axis_size("dp")), "dp", 0, 0), axis=2
+        ),
         preferred_element_type=jnp.float32,
     )
     hidden = hidden_units(partial_value)

time: 749 us -> 834 us (1.11)
  waiting for transfers between devices: 472 us -> 522 us
  local copies, waits for them, and re-layouts: 0.69 us -> 22.7 us
  starting transfers between devices: 0.2 us -> 10.6 us
    all_to_all x0 -> x1, waiting for transfers between devices: none -> 321 us  [per_device(): lax.all_to_all(jnp.stack([gate_up] * lax.axis_size('dp')), 'dp', 0, 0)]
    all_gather x1 -> x0, waiting for transfers between devices: 192 us -> none  [per_device(): lax.all_gather(gate_up, 'dp', axis=2, tiled=True)]
    all_gather x1, waiting for transfers between devices: 127 us -> 0.02 us  [per_device(): lax.all_gather(down_weight, 'dp', axis=0, tiled=True)]
    reduce_scatter x1, waiting for transfers between devices: 113 us -> 159 us  [hidden_units(): lax.psum_scatter(partial_value, 'row', scatter_dimension=0, tiled=True)]
    all_to_all x0 -> x1, local copies, waits for them, and re-layouts: none -> 13.7 us  [per_device(): lax.all_to_all(jnp.stack([gate_up] * lax.axis_size('dp')), 'dp', 0, 0)]
    all_to_all x0 -> x1, starting transfers between devices: none -> 10.5 us  [per_device(): lax.all_to_all(jnp.stack([gate_up] * lax.axis_size('dp')), 'dp', 0, 0)]
  transfers between devices with their start and end apart: 5 -> 5, of which waited for: 4 -> 3; matrix products, arithmetic and copies ran while one was open for 2% -> 2% of each run, Pallas kernels for 0% -> 0%
where the time goes in v2:
time: 834 us; the launch traced here: 833 us
  waiting for transfers between devices  522 us (63%)
  blocking collectives  212 us (25%)
  matrix products  38.6 us (5%)
  local copies, waits for them, and re-layouts  22.7 us (3%)
  between operations  16.4 us (2%)
  other arithmetic  10.9 us (1%)
  starting transfers between devices  10.6 us (1%)
    all_to_all x1, waiting for transfers between devices, per_device(): lax.all_to_all(jnp.stack([gate_up] * lax.axis_size('dp')), 'dp', 0, 0)  321 us
    psum x1, blocking collectives, per_device(): col_check = lax.psum(column_part, ('dp', 'col')) / math.sqrt(total_tokens)  180 us
    reduce_scatter x1, waiting for transfers between devices, hidden_units(): lax.psum_scatter(partial_value, 'row', scatter_dimension=0, tiled=True)  159 us
    all_gather x1, waiting for transfers between devices, hidden_units(): return lax.all_gather(swiglu(share), 'row', axis=0, tiled=True)  41.8 us
    dot_general x1, matrix products, per_device(): jnp.einsum('td,gdf->tgf', group_rows, jnp.concatenate(lax.all_to_all(jnp....  22.1 us
  transfers between devices with their start and end apart: 5, of which 3 were waited for; matrix products, arithmetic and copies ran while one was open for 2% of the time, Pallas kernels for 0%

profile of v2, /device:TPU:8, one launch (start us, length us, event | category | flops | bytes accessed | tf_op | source)
XLA Modules:
  0.0 833.3 jit_solution(11264085320544359734)
XLA Ops:
  8.0 8.3 stack.2
  16.3 0.0 copy-start.1
  16.3 10.5 %all-to-all-start = ((bf16[16,2,1024,224]{2,3,1,0:T(8,128)(2,1)}), bf16[16,2,1024,224]{2,3,1,0:T(8,128)(2,1)}, u32[]{:S(2)}, u32[]{:S(2)}) async-start(bf16[16,2,1024,224]{2,3,1,0:T(8,128)(2,1)} %stack.2), calls=%async_computation | async-start | bytes 29360128 | tf_op jit(solution)/shard_map/all_to_all | solution.py:36
  26.7 0.0 reduce-scatter.3.cloned.1.call-start
  26.8 0.0 copy-done.1
  26.8 14.0 %all_gather.9 = bf16[448,1024]{1,0:T(8,128)(2,1)S(1)} all-gather(bf16[112,1024]{1,0:T(8,128)(2,1)S(1)} %copy-done.1), channel_id=1, replica_groups=mesh['dp'=16,'row'=4,'col'=4] {'col'}, dimensions={0}, use_global_device_ids=true | all-gather | bytes 1146880 | tf_op jit(solution)/shard_map/all_gather | solution.py:31
  40.9 320.7 %all-to-all-done = bf16[16,2,1024,224]{2,3,1,0:T(8,128)(2,1)} async-done(((bf16[16,2,1024,224]{2,3,1,0:T(8,128)(2,1)}), bf16[16,2,1024,224]{2,3,1,0:T(8,128)(2,1)}, u32[]{:S(2)}, u32[]{:S(2)}) %all-to-all-start) | async-done | bytes 14680096 | tf_op jit(solution)/shard_map/all_to_all | solution.py:36
  361.5 13.7 %copy.8 = bf16[16,2,1024,224]{2,3,0,1:T(8,128)(2,1)} copy(bf16[16,2,1024,224]{2,3,1,0:T(8,128)(2,1)} %all-to-all-done) | data formatting | bytes 29360128 | tf_op jit(solution)/shard_map/all_to_all | solution.py:36
  375.2 22.1 %fusion.2 = f32[448,2,3584]{2,0,1:T(8,128)} fusion(bf16[2,1024,3584]{1,2,0:T(8,128)(2,1)} %bitcast.26, bf16[448,1024]{1,0:T(8,128)(2,1)S(1)} %all_gather.9), kind=kOutput, calls=%fused_computation.6 | convolution fusion | flops 6576668672 | bytes 28442624 | tf_op jit(solution)/shard_map/td,gdf->tgf/dot_general | solution.py:32
  397.3 0.0 reduce-scatter.3.cloned.1.call-update
  397.3 0.0 all-gather.5.cloned.1.call-start
  397.4 0.5 all-gather.5.cloned.1.call-update
  397.9 0.0 all-gather.3.cloned.1.call-start
  398.0 159.3 %reduce-scatter.3.cloned.1.call-done = f32[112,2,3584]{2,0,1:T(8,128)} async-done(((f32[448,2,3584]{2,0,1:T(8,128)}), f32[112,2,3584]{2,0,1:T(8,128)}) %reduce-scatter.3.cloned.1.call-update) | async-done | bytes 3211280 | tf_op jit(solution)/shard_map/reduce_scatter | solution.py:13
  557.3 3.2 fusion.1
  560.5 0.0 all-gather.3.cloned.1.call-update
  560.5 0.0 copy-start.2
  560.5 0.0 reduce-scatter.5.cloned.1.call-start
  560.6 0.0 all-gather.5.cloned.1.call-done
  560.6 41.8 %all-gather.3.cloned.1.call-done = bf16[448,3584]{1,0:T(8,128)(2,1)} async-done(((bf16[112,3584]{1,0:T(8,128)(2,1)}), bf16[448,3584]{1,0:T(8,128)(2,1)}) %all-gather.3.cloned.1.call-update) | async-done | bytes 3211280 | tf_op jit(solution)/shard_map/all_gather | solution.py:14
  602.4 8.8 %fusion.4 = f32[448,1024]{1,0:T(8,128)} fusion(bf16[448,3584]{1,0:T(8,128)(2,1)} %all-gather.3.cloned.1.call-done, bf16[3584,1024]{1,0:T(8,128)(2,1)} %all-gather.5.cloned.1.call-done), kind=kOutput, calls=%fused_computation.10 | convolution fusion | flops 3288334336 | bytes 12386304 | tf_op jit(solution)/shard_map/dot_general | solution.py:20
  611.2 0.0 reduce-scatter.5.cloned.1.call-update
  611.2 0.0 copy-done.2
  611.2 0.6 dynamic-slice
  612.4 0.0 copy-start
  612.4 4.3 convert_reduce_fusion
  616.7 0.0 copy-done
  616.7 0.6 convert_reduce_fusion.1
  617.3 2.6 fusion.6
  619.9 10.8 %all-reduce = f32[448]{0:T(512)S(1)} all-reduce(f32[448]{0:T(512)S(1)} %bitcast.28), channel_id=4, replica_groups=mesh['dp'=16,'row'=4,'col'=4] {'col'}, use_global_device_ids=true, to_apply=%region_5.6.clone | all-reduce | flops 448 | bytes 3584
  630.7 0.1 dynamic-slice.1
  630.8 6.6 psum.15
  637.4 5.1 fusion.5
  642.5 180.3 %psum.14 = f32[1024]{0:T(1024)S(1)} all-reduce(f32[1024]{0:T(1024)S(1)} %bitcast.27), channel_id=1, replica_groups=mesh['dp'=16,'row'=4,'col'=4] {'dp','col'}, use_global_device_ids=true, to_apply=%region_3.4 | all-reduce | flops 1024 | bytes 8192 | tf_op jit(solution)/shard_map/psum | solution.py:48
  822.8 0.5 broadcast_multiply_fusion.1
  823.3 0.6 broadcast_multiply_fusion
  823.9 0.0 reduce-scatter.5.cloned.1.call-done
  823.9 1.7 convert_element_type.13
  (2 shorter events, 0.0 us)
Async XLA Ops:
  16.3 10.5 %copy-start.1 = (bf16[112,1024]{1,0:T(8,128)(2,1)S(1)}, bf16[112,1024]{1,0:T(8,128)(2,1)}, u32[]{:S(2)}) copy-start(bf16[112,1024]{1,0:T(8,128)(2,1)} %param.3) | copy-start | bytes 688132
  16.3 345.3 %all-to-all-start = ((bf16[16,2,1024,224]{2,3,1,0:T(8,128)(2,1)}), bf16[16,2,1024,224]{2,3,1,0:T(8,128)(2,1)}, u32[]{:S(2)}, u32[]{:S(2)}) async-start(bf16[16,2,1024,224]{2,3,1,0:T(8,128)(2,1)} %stack.2), calls=%async_computation | async-start | bytes 29360128 | tf_op jit(solution)/shard_map/all_to_all | solution.py:36
  26.7 530.5 %reduce-scatter.3.cloned.1.call-start = ((), (), s32[]{:S(2)}) async-start(), calls=%async_computation.3 | async-start | bytes 16056320 | tf_op jit(solution)/shard_map/reduce_scatter | solution.py:13
  397.3 163.3 %all-gather.5.cloned.1.call-start = ((), (), s32[]{:S(2)}) async-start(), calls=%async_computation.5 | async-start | bytes 7798784 | tf_op jit(solution)/shard_map/all_gather | solution.py:42
  397.9 204.4 %all-gather.3.cloned.1.call-start = ((), (), s32[]{:S(2)}) async-start(), calls=%async_computation.4 | async-start | bytes 4014080 | tf_op jit(solution)/shard_map/all_gather | solution.py:14
  560.5 50.7 %copy-start.2 = (u32[256]{0:T(256)S(1)}, u32[256]{0:T(256)}, u32[]{:S(2)}) copy-start(u32[256]{0:T(256)} %constant.16) | copy-start | bytes 3076
  560.5 263.4 %reduce-scatter.5.cloned.1.call-start = ((), (), s32[]{:S(2)}) async-start(), calls=%async_computation.6 | async-start | bytes 2293760 | tf_op jit(solution)/shard_map/reduce_scatter | solution.py:45
  612.4 4.3 copy-start
Sparse Core Ops, SparseCore 0:
  397.5 159.7 reduce-scatter.2
Sparse Core Ops, SparseCore 1:
  400.4 148.7 all-gather.4
  560.6 41.7 all-gather.2
  611.3 32.6 reduce-scatter.4
